TPU v7x, 32 devices: a whole 2x2x4 slice. The times are simulated.
32 devices in a mesh: batch: 4 (over z), token: 8 (over y, x, core).
Axes of the slice: x: 2, y: 2, z: 4, core: 2. Of those that a mesh axis runs over, the one named last changes fastest.
Arguments:
- tokens: bfloat16 [16384, 768], P(('batch', 'token')), may hold values from -9 to 9
- slot_weight: bfloat16 [768, 1024], replicated, may hold values from -2 to 2
- expert_in: bfloat16 [128, 768, 3072], P('token', None, 'batch'), may hold values from -1.7265625 to 1.7265625
- expert_out: bfloat16 [128, 3072, 768], P('token', 'batch'), may hold values from -0.6484375 to 0.6484375
Outputs:
- mixed: bfloat16 [16384, 768], P(('batch', 'token'))
All inputs are finite; a program needn't handle non-finite values.
Results may differ from a plain program's by a relative error of at most 0.023.
Values may be sent and summed in bfloat16 or wider, within the bound.
No kernel may reach another device: no remote copies, remote signals or barrier semaphores. Data moves between devices by JAX's collectives and lax.ppermute only.
A program may use at most 128 MiB of HBM per device.

v0:
```python
import jax
import jax.numpy as jnp
from jax import lax
from jax.sharding import PartitionSpec as P


def body(tokens, slot_weight, expert_in, expert_out):
    widened = tokens.astype(jnp.float32)
    scale_row = lax.rsqrt(jnp.mean(widened * widened, axis=-1, keepdims=True) + 1e-06)
    normed = (widened * scale_row).astype(jnp.bfloat16)
    logits = jnp.dot(normed, slot_weight, preferred_element_type=jnp.float32)
    column_max = lax.pmax(jnp.max(logits, axis=0), "token")
    raised = jnp.exp(logits - column_max[None, :])
    column_sum = lax.psum(jnp.sum(raised, axis=0), "token")
    dispatch = raised.astype(jnp.bfloat16)
    partial_value = jnp.einsum("ts,td->sd", dispatch, normed, preferred_element_type=jnp.float32)
    own_count = slot_weight.shape[1] // lax.axis_size("token")
    offset = lax.axis_index("token") * own_count
    own_rows = lax.psum_scatter(
        partial_value.astype(jnp.bfloat16), "token", scatter_dimension=0, tiled=True
    ).astype(jnp.float32)
    own_total = lax.dynamic_slice_in_dim(column_sum, offset, own_count, 0)
    experts_here = expert_in.shape[0]
    slot_inputs = (own_rows / own_total[:, None]).astype(jnp.bfloat16)
    slot_inputs = slot_inputs.reshape(experts_here, own_count // experts_here, tokens.shape[1])
    hidden = jnp.einsum(
        "esd,edf->esf",
        lax.all_gather(slot_inputs, "batch", axis=1, tiled=True),
        expert_in,
        preferred_element_type=jnp.float32,
    )
    hidden = jax.nn.gelu(hidden, approximate=False).astype(jnp.bfloat16)
    terms = jnp.einsum("esf,efd->esd", hidden, expert_out, preferred_element_type=jnp.float32)
    slot_outputs = lax.psum_scatter(
        terms.astype(jnp.bfloat16), "batch", scatter_dimension=1, tiled=True
    )
    combine = jax.nn.softmax(logits, axis=1).astype(jnp.bfloat16)
    slots_each = slot_outputs.shape[1]
    block_rows = lax.all_gather(slot_outputs, "token", axis=0, tiled=True)
    number = block_rows.shape[0]
    flat_rows = block_rows.reshape(number * slots_each, block_rows.shape[2])
    mixed = jnp.dot(combine, flat_rows, preferred_element_type=jnp.float32)
    return mixed.astype(jnp.bfloat16)


def solution(mesh):
    placed = (
        P(("batch", "token"), None),
        P(),
        P("token", None, "batch"),
        P("token", "batch", None),
    )
    return jax.shard_map(
        body, mesh=mesh, in_specs=placed, out_specs=P(("batch", "token"), None), check_vma=False
    )
```

profile of v0, /device:TPU:0, one launch (start us, length us, event | category | flops | bytes accessed | tf_op | source)
XLA Modules:
  0.0 166.7 jit_solution(7911845399044545035)
XLA Ops:
  6.5 0.0 copy-start
  6.5 0.0 reduce-scatter.5.cloned.1.call-start
  6.5 1.5 fusion.3
  8.0 0.1 copy-done
  8.2 0.0 copy-start.1
  8.2 3.6 %fusion.93 = (f32[512]{0:T(512)S(1)}, f32[1024]{0:T(1024)S(1)}, f32[512,1024]{1,0:T(8,128)}) fusion(bf16[768,1024]{1,0:T(8,128)(2,1)S(1)} %copy-done, bf16[512,768]{1,0:T(8,128)(2,1)} %param.4, f32[512]{0:T(512)S(1)} %add_rsqrt_fusion), kind=kOutput, calls=%fused_computation.110 | convolution fusion | flops 807533056 | bytes 4464640 | tf_op jit(solution)/shard_map/dot_general | solution.py:11
  11.8 15.1 %pmax.7 = f32[1024]{0:T(1024)S(1)} all-reduce(f32[1024]{0:T(1024)S(1)} %get-tuple-element.8), channel_id=1, replica_groups=mesh['batch'=4,'token'=8] {'token'}, use_global_device_ids=true, to_apply=%region_4.0 | all-reduce | flops 1024 | bytes 8192 | tf_op jit(solution)/shard_map/pmax | solution.py:12
  26.9 0.0 copy-done.1
  26.9 3.9 %convolution_convert_fusion = bf16[1024,768]{1,0:T(8,128)(2,1)} fusion(f32[512,1024]{1,0:T(8,128)} %get-tuple-element.11, f32[1024]{0:T(1024)S(1)} %pmax.7, bf16[512,768]{1,0:T(8,128)(2,1)S(1)} %copy-done.1, f32[512]{0:T(512)S(1)} %add_rsqrt_fusion), kind=kOutput, calls=%fused_computation.9 | convolution fusion | flops 808321024 | bytes 4462592 | tf_op jit(solution)/shard_map/ts,td->sd/dot_general | solution.py:16
  30.8 0.0 reduce-scatter.5.cloned.1.call-update
  30.8 0.0 reduce-scatter.7.cloned.1.call-start
  30.8 2.3 %fusion = (f32[512]{0:T(512)S(1)}, f32[1024]{0:T(1024)S(1)}) fusion(f32[512,1024]{1,0:T(8,128)} %get-tuple-element.11, f32[512]{0:T(512)S(1)} %get-tuple-element.7, f32[1024]{0:T(1024)S(1)} %pmax.7), kind=kLoop, calls=%fused_computation.6 | loop fusion | flops 2095616 | bytes 2109440 | tf_op jit(solution)/shard_map/reduce_sum | solution.py:37
  33.1 11.8 %psum.7 = f32[1024]{0:T(1024)S(1)} all-reduce(f32[1024]{0:T(1024)S(1)} %get-tuple-element.6), channel_id=1, replica_groups=mesh['batch'=4,'token'=8] {'token'}, use_global_device_ids=true, to_apply=%region_7.0 | all-reduce | flops 1024 | bytes 8192 | tf_op jit(solution)/shard_map/psum | solution.py:14
  44.9 0.1 dynamic_slice.3
  45.0 23.6 %reduce-scatter.5.cloned.1.call-done = bf16[128,768]{1,0:T(8,128)(2,1)} async-done(((bf16[1024,768]{1,0:T(8,128)(2,1)}), bf16[128,768]{1,0:T(8,128)(2,1)}) %reduce-scatter.5.cloned.1.call-update) | async-done | bytes 196624 | tf_op jit(solution)/shard_map/reduce_scatter | solution.py:19
  68.7 1.0 fusion.61
  69.7 19.6 %all_gather.6 = bf16[16,32,768]{2,1,0:T(8,128)(2,1)S(1)} all-gather(bf16[16,8,768]{2,1,0:T(8,128)(2,1)S(1)} %fusion.61), channel_id=1, replica_groups=mesh['batch'=4,'token'=8] {'batch'}, dimensions={1}, use_global_device_ids=true | all-gather | bytes 983040 | tf_op jit(solution)/shard_map/all_gather | solution.py:28
  89.3 8.1 %fusion.55 = (u16[32,768]{1,0:T(8,128)(2,1)S(1)}, u16[32,768]{1,0:T(8,128)(2,1)S(1)}, f32[16,32,768]{2,1,0:T(8,128)S(1)}) fusion(bf16[16,32,768]{2,1,0:T(8,128)(2,1)S(1)} %all_gather.6, bf16[16,768,768]{2,1,0:T(8,128)(2,1)} %param.6), kind=kOutput, calls=%fused_computation.71 | convolution fusion | flops 609042432 | bytes 21331968 | tf_op jit(solution)/shard_map/esd,edf->esf/dot_general | solution.py:26
  97.4 9.0 %fusion.94 = bf16[4,8,16,768]{3,1,0,2:T(8,128)(2,1)S(1)} fusion(bf16[16,768,768]{2,1,0:T(8,128)(2,1)} %param.7, f32[16,32,768]{2,1,0:T(8,128)S(1)} %get-tuple-element.12, u16[32,768]{1,0:T(8,128)(2,1)S(1)} %get-tuple-element.10, u16[32,768]{1,0:T(8,128)(2,1)S(1)} %get-tuple-element.9), kind=kOutput, calls=%fused_computation.111 | convolution fusion | flops 631898112 | bytes 21331968 | tf_op jit(solution)/shard_map/esf,efd->esd/dot_general | solution.py:33
  106.5 0.9 copy.7
  107.4 0.0 reduce-scatter.7.cloned.1.call-update
  107.4 0.0 all-gather.2.cloned.1.call-start
  107.5 21.8 %reduce-scatter.7.cloned.1.call-done = bf16[8,12288]{1,0:T(8,128)(2,1)} async-done(((bf16[32,12288]{1,0:T(8,128)(2,1)}), bf16[8,12288]{1,0:T(8,128)(2,1)}) %reduce-scatter.7.cloned.1.call-update) | async-done | bytes 196624
  129.2 1.0 copy.11
  130.2 0.7 copy.6
  130.9 0.0 all-gather.2.cloned.1.call-update
  131.0 25.3 %all-gather.2.cloned.1.call-done = bf16[128,8,768]{2,1,0:T(8,128)(2,1)} async-done(((bf16[16,8,768]{2,1,0:T(8,128)(2,1)}), bf16[128,8,768]{2,1,0:T(8,128)(2,1)}) %all-gather.2.cloned.1.call-update) | async-done | bytes 1572880 | tf_op jit(solution)/shard_map/all_gather | solution.py:39
  156.2 4.0 %fusion.16 = bf16[512,768]{1,0:T(8,128)(2,1)} fusion(bf16[128,8,768]{2,1,0:T(8,128)(2,1)} %all-gather.2.cloned.1.call-done, f32[512,1024]{1,0:T(8,128)} %get-tuple-element.11, f32[512]{0:T(512)S(1)} %get-tuple-element.5, f32[512]{0:T(512)S(1)} %get-tuple-element.7), kind=kOutput, calls=%fused_computation.35 | convolution fusion | flops 807272448 | bytes 4460544 | tf_op jit(solution)/shard_map/dot_general | solution.py:42
  (1 shorter events, 0.0 us)
Async XLA Ops:
  6.5 1.6 copy-start
  6.5 62.1 %reduce-scatter.5.cloned.1.call-start = ((), (), s32[]{:S(2)}) async-start(), calls=%async_computation.2 | async-start | bytes 1769472 | tf_op jit(solution)/shard_map/reduce_scatter | solution.py:19
  8.2 18.7 %copy-start.1 = (bf16[512,768]{1,0:T(8,128)(2,1)S(1)}, bf16[512,768]{1,0:T(8,128)(2,1)}, u32[]{:S(2)}) copy-start(bf16[512,768]{1,0:T(8,128)(2,1)} %param.4) | copy-start | bytes 2359300
  30.8 98.4 %reduce-scatter.7.cloned.1.call-start = ((), (), s32[]{:S(2)}) async-start(), calls=%async_computation.4 | async-start | bytes 983040
  107.4 48.8 %all-gather.2.cloned.1.call-start = ((), (), s32[]{:S(2)}) async-start(), calls=%async_computation.3 | async-start | bytes 1769472 | tf_op jit(solution)/shard_map/all_gather | solution.py:39
Sparse Core Ops, SparseCore 0:
  30.9 37.7 reduce-scatter.4
  107.5 21.6 reduce-scatter.6
  131.1 25.0 all-gather.1
where the time goes:
time: 167 us
  waiting for transfers between devices  70.7 us (42%)
  blocking collectives  46.5 us (28%)
  matrix products  28.6 us (17%)
  between operations  13.1 us (8%)
  other arithmetic  4.83 us (3%)
  local copies, waits for them, and re-layouts  2.86 us (2%)
    all_gather x1, waiting for transfers between devices, body(): block_rows = lax.all_gather(slot_outputs, 'token', axis=0, tiled=True)  25.3 us
    reduce_scatter x1, waiting for transfers between devices, body(): lax.psum_scatter(partial_value.astype(jnp.bfloat16), 'token', scatter_dim...  23.6 us
    unnamed x4, waiting for transfers between devices  21.8 us
    all_gather x1, blocking collectives, body(): lax.all_gather(slot_inputs, 'batch', axis=1, tiled=True)  19.6 us
    pmax x1, blocking collectives, body(): column_max = lax.pmax(jnp.max(logits, axis=0), 'token')  15.1 us
    psum x1, blocking collectives, body(): column_sum = lax.psum(jnp.sum(raised, axis=0), 'token')  11.8 us
    dot_general x1, matrix products, body(): jnp.einsum('esf,efd->esd', hidden, expert_out, preferred_element_type=jnp...  9.04 us
    dot_general x1, matrix products, body(): jnp.einsum('esd,edf->esf', lax.all_gather(slot_inputs, 'batch', axis=1, t...  8.12 us
  transfers between devices with their start and end apart: 3, of which 3 were waited for; matrix products, arithmetic and copies ran while one was open for 1% of the time, Pallas kernels for 0%

commit v1 on v0

--- a/solution.py
+++ b/solution.py
@@ -2,6 +2,41 @@
 import jax.numpy as jnp
 from jax import lax
 from jax.sharding import PartitionSpec as P
+
+
+def spread_frame(unit, d0, packet, d_out):
+    u_next = lax.axis_size("batch")
+    state_now = lax.axis_index("batch")
+    y_new, o_now, k_now = (u_next, state_now, unit.shape[d0])
+    out_arr = map(lambda c: (c, (c + 1) % y_new), range(y_new))
+    store = list(out_arr)
+    found = [(pp, kk) for kk, pp in store]
+    main = lax.ppermute(unit, "batch", store)
+    response = lax.ppermute(unit, "batch", found)
+    y, q_next = (main, response)
+    tmp = packet(unit, o_now * k_now)
+    m_next = tmp.shape[d_out]
+    y1 = jnp.zeros((*tmp.shape[:d_out], y_new * m_next, *tmp.shape[d_out + 1 :]), tmp.dtype)
+
+    def obtain_layers_all_in(y1, tmp, parts_out):
+        return lax.dynamic_update_slice_in_dim(y1, tmp, parts_out * m_next, axis=d_out)
+
+    y1 = obtain_layers_all_in(y1, tmp, o_now)
+    s = 1
+    while s < y_new // 2 + 1:
+        z, base_arr = ((o_now - s) % y_new, (o_now + s) % y_new)
+        e_next = (y, q_next)
+        if s < y_new // 2:
+            outcome_arr = lax.ppermute(y, "batch", store)
+            top = lax.ppermute(q_next, "batch", found)
+            y, q_next = (outcome_arr, top)
+        w_next = packet(e_next[0], z * k_now)
+        y1 = obtain_layers_all_in(y1, w_next, z)
+        if 2 * s < y_new:
+            left_arr = packet(e_next[1], base_arr * k_now)
+            y1 = obtain_layers_all_in(y1, left_arr, base_arr)
+        s = s + 1
+    return y1
 
 
 def body(tokens, slot_weight, expert_in, expert_out):
@@ -23,11 +58,13 @@
     experts_here = expert_in.shape[0]
     slot_inputs = (own_rows / own_total[:, None]).astype(jnp.bfloat16)
     slot_inputs = slot_inputs.reshape(experts_here, own_count // experts_here, tokens.shape[1])
-    hidden = jnp.einsum(
-        "esd,edf->esf",
-        lax.all_gather(slot_inputs, "batch", axis=1, tiled=True),
-        expert_in,
-        preferred_element_type=jnp.float32,
+    hidden = spread_frame(
+        slot_inputs,
+        1,
+        lambda part, start: jnp.einsum(
+            "esd,edf->esf", part, expert_in, preferred_element_type=jnp.float32
+        ),
+        1,
     )
     hidden = jax.nn.gelu(hidden, approximate=False).astype(jnp.bfloat16)
     terms = jnp.einsum("esf,efd->esd", hidden, expert_out, preferred_element_type=jnp.float32)

time: 167 us -> 167 us (level)
  blocking collectives: 46.5 us -> 27 us
  matrix products: 28.6 us -> 42.3 us
  starting transfers between devices: 0.09 us -> 4.2 us
    all_gather x1 -> x0, blocking collectives: 19.6 us -> none  [body(): lax.all_gather(slot_inputs, 'batch', axis=1, tiled=True)]
    dot_general x1 -> x4, matrix products: 8.12 us -> 21.9 us  [body(): jnp.einsum('esd,edf->esf', part, expert_in, preferred_element_type=jnp.fl...]
    ppermute x0 -> x3, starting transfers between devices: none -> 4.12 us  [the longest x1 2.34 us: spread_frame(): response = lax.ppermute(unit, 'batch', found)]
  transfers between devices with their start and end apart: 3 -> 6, of which waited for: 3 -> 3; matrix products, arithmetic and copies ran while one was open for 1% -> 13% of each run, Pallas kernels for 0% -> 0%
where the time goes in v1:
time: 167 us
  waiting for transfers between devices  71.8 us (43%)
  matrix products  42.3 us (25%)
  blocking collectives  27 us (16%)
  between operations  13.3 us (8%)
  other arithmetic  4.83 us (3%)
  starting transfers between devices  4.2 us (3%)
  local copies, waits for them, and re-layouts  3.32 us (2%)
    all_gather x1, waiting for transfers between devices, body(): block_rows = lax.all_gather(slot_outputs, 'token', axis=0, tiled=True)  25.3 us
    reduce_scatter x1, waiting for transfers between devices, body(): lax.psum_scatter(partial_value.astype(jnp.bfloat16), 'token', scatter_dim...  23.5 us
    unnamed x4, waiting for transfers between devices  23 us
    dot_general x4, matrix products, body(): jnp.einsum('esd,edf->esf', part, expert_in, preferred_element_type=jnp.fl...  21.9 us
    pmax x1, blocking collectives, body(): column_max = lax.pmax(jnp.max(logits, axis=0), 'token')  15.2 us
    psum x1, blocking collectives, body(): column_sum = lax.psum(jnp.sum(raised, axis=0), 'token')  11.8 us
    dot_general x1, matrix products, body(): jnp.einsum('esf,efd->esd', hidden, expert_out, preferred_element_type=jnp...  8.93 us
    dot_general x1, matrix products, body(): mixed = jnp.dot(combine, flat_rows, preferred_element_type=jnp.float32)  4 us
  transfers between devices with their start and end apart: 6, of which 3 were waited for; matrix products, arithmetic and copies ran while one was open for 13% of the time, Pallas kernels for 0%

profile of v1, /device:TPU:0, one launch (start us, length us, event | category | flops | bytes accessed | tf_op | source)
XLA Modules:
  0.0 166.7 jit_solution(3083478716375110683)
XLA Ops:
  6.5 1.5 fusion.3
  8.0 0.1 copy-done
  8.2 3.6 %fusion.88 = (f32[512]{0:T(512)S(1)}, f32[1024]{0:T(1024)S(1)}, f32[512,1024]{1,0:T(8,128)}) fusion(bf16[768,1024]{1,0:T(8,128)(2,1)S(1)} %copy-done, bf16[512,768]{1,0:T(8,128)(2,1)} %param.4, f32[512]{0:T(512)S(1)} %add_rsqrt_fusion), kind=kOutput, calls=%fused_computation.105 | convolution fusion | flops 807533056 | bytes 4464640 | tf_op jit(solution)/shard_map/dot_general | solution.py:46
  11.8 15.2 %pmax.7 = f32[1024]{0:T(1024)S(1)} all-reduce(f32[1024]{0:T(1024)S(1)} %get-tuple-element.8), channel_id=1, replica_groups=mesh['batch'=4,'token'=8] {'token'}, use_global_device_ids=true, to_apply=%region_4.0 | all-reduce | flops 1024 | bytes 8192 | tf_op jit(solution)/shard_map/pmax | solution.py:47
  26.9 3.9 %convolution_convert_fusion = bf16[1024,768]{1,0:T(8,128)(2,1)} fusion(f32[512,1024]{1,0:T(8,128)} %get-tuple-element.9, f32[1024]{0:T(1024)S(1)} %pmax.7, bf16[512,768]{1,0:T(8,128)(2,1)S(1)} %copy-done.1, f32[512]{0:T(512)S(1)} %add_rsqrt_fusion), kind=kOutput, calls=%fused_computation.9 | convolution fusion | flops 808321024 | bytes 4462592 | tf_op jit(solution)/shard_map/ts,td->sd/dot_general | solution.py:51
  30.8 0.0 reduce-scatter.5.cloned.1.call-update
  30.8 0.0 reduce-scatter.7.cloned.1.call-start
  30.9 2.3 %fusion = (f32[512]{0:T(512)S(1)}, f32[1024]{0:T(1024)S(1)}) fusion(f32[512,1024]{1,0:T(8,128)} %get-tuple-element.9, f32[512]{0:T(512)S(1)} %get-tuple-element.7, f32[1024]{0:T(1024)S(1)} %pmax.7), kind=kLoop, calls=%fused_computation.6 | loop fusion | flops 2095616 | bytes 2109440 | tf_op jit(solution)/shard_map/reduce_sum | solution.py:74
  33.2 11.8 %psum.7 = f32[1024]{0:T(1024)S(1)} all-reduce(f32[1024]{0:T(1024)S(1)} %get-tuple-element.6), channel_id=1, replica_groups=mesh['batch'=4,'token'=8] {'token'}, use_global_device_ids=true, to_apply=%region_7.8 | all-reduce | flops 1024 | bytes 8192 | tf_op jit(solution)/shard_map/psum | solution.py:49
  45.0 0.1 dynamic_slice.3
  45.1 23.5 %reduce-scatter.5.cloned.1.call-done = bf16[128,768]{1,0:T(8,128)(2,1)} async-done(((bf16[1024,768]{1,0:T(8,128)(2,1)}), bf16[128,768]{1,0:T(8,128)(2,1)}) %reduce-scatter.5.cloned.1.call-update) | async-done | bytes 196624 | tf_op jit(solution)/shard_map/reduce_scatter | solution.py:54
  68.6 1.0 fusion.57
  69.7 1.5 collective-permute-start
  71.2 2.3 %collective-permute-start.1 = (bf16[16,8,768]{2,1,0:T(8,128)(2,1)S(1)}, bf16[16,8,768]{2,1,0:T(8,128)(2,1)S(1)}, u32[]{:S(2)}, u32[]{:S(2)}) collective-permute-start(bf16[16,8,768]{2,1,0:T(8,128)(2,1)S(1)} %fusion.57), channel_id=1, source_target_pairs={{8,0},{16,8},{24,16},{0,24},{9,1},{17,9},{25,17},{1,25},{10,2},{18... | collective-permute-start | bytes 589832 | tf_op jit(solution)/shard_map/ppermute | solution.py:15
  73.6 0.1 broadcast.24
  73.7 8.6 %convolution_dynamic-update-slice_fusion.3 = f32[16,32,768]{2,1,0:T(8,128)S(1)} fusion(f32[16,32,768]{2,1,0:T(8,128)S(1)} %broadcast.24, s32[]{:T(128)S(6)} %select_n.31, bf16[16,8,768]{2,1,0:T(8,128)(2,1)S(1)} %fusion.57, bf16[16,768,768]{2,1,0:T(8,128)(2,1)} %param.6), kind=kOutput, calls=%fused_computation.37 | convolution fusion | flops 150994944 | bytes 19464196 | tf_op jit(solution)/shard_map/esd,edf->esf/dot_general | solution.py:64
  82.3 0.0 collective-permute-done
  82.3 0.2 collective-permute-start.2
  82.6 8.2 %convolution_dynamic-update-slice_fusion.2 = f32[16,32,768]{2,1,0:T(8,128)S(1)} fusion(f32[16,32,768]{2,1,0:T(8,128)S(1)} %convolution_dynamic-update-slice_fusion.3, s32[]{:T(128)S(6)} %select_n.33, bf16[16,8,768]{2,1,0:T(8,128)(2,1)S(1)} %collective-permute-done, bf16[16,768,768]{2,1,0:T(8,128)(2,1)} %param.6), kind=kOutput, calls=%fused_computation.36 | convolution fusion | flops 150994944 | bytes 19464196 | tf_op jit(solution)/shard_map/esd,edf->esf/dot_general | solution.py:64
  90.8 0.3 slice-done.4
  91.1 2.5 %convolution_dynamic-update-slice_fusion.1 = f32[16,32,768]{2,1,0:T(8,128)S(1)} fusion(f32[16,32,768]{2,1,0:T(8,128)S(1)} %convolution_dynamic-update-slice_fusion.2, s32[]{:T(128)S(6)} %select_n.35, bf16[16,8,768]{2,1,0:T(8,128)(2,1)S(1)} %collective-permute-done.1, bf16[16,768,768]{2,1,0:T(8,128)(2,1)S(1)} %bitcast.30), kind=kOutput, calls=%fused_computation.35 | convolution fusion | flops 150994944 | bytes 19464196 | tf_op jit(solution)/shard_map/esd,edf->esf/dot_general | solution.py:64
  93.7 2.5 %convolution_dynamic-update-slice_fusion = f32[16,32,768]{2,1,0:T(8,128)S(1)} fusion(f32[16,32,768]{2,1,0:T(8,128)S(1)} %convolution_dynamic-update-slice_fusion.1, s32[]{:T(128)S(6)} %select_n.37, bf16[16,8,768]{2,1,0:T(8,128)(2,1)S(1)} %collective-permute-done.2, bf16[16,768,768]{2,1,0:T(8,128)(2,1)S(1)} %bitcast.30), kind=kOutput, calls=%fused_computation.34 | convolution fusion | flops 150994944 | bytes 19464196 | tf_op jit(solution)/shard_map/esd,edf->esf/dot_general | solution.py:64
  96.2 8.9 %fusion.89 = bf16[4,8,16,768]{3,1,0,2:T(8,128)(2,1)S(1)} fusion(bf16[16,768,768]{2,1,0:T(8,128)(2,1)} %param.7, f32[16,32,768]{2,1,0:T(8,128)S(1)} %convolution_dynamic-update-slice_fusion), kind=kOutput, calls=%fused_computation.106 | convolution fusion | flops 629932032 | bytes 21233664 | tf_op jit(solution)/shard_map/esf,efd->esd/dot_general | solution.py:70
  105.2 0.9 copy.7
  106.1 0.0 reduce-scatter.7.cloned.1.call-update
  106.1 0.0 all-gather.2.cloned.1.call-start
  106.2 23.0 %reduce-scatter.7.cloned.1.call-done = bf16[8,12288]{1,0:T(8,128)(2,1)} async-done(((bf16[32,12288]{1,0:T(8,128)(2,1)}), bf16[8,12288]{1,0:T(8,128)(2,1)}) %reduce-scatter.7.cloned.1.call-update) | async-done | bytes 196624
  129.1 1.0 copy.11
  130.1 0.7 copy.6
  130.8 0.0 all-gather.2.cloned.1.call-update
  130.9 25.3 %all-gather.2.cloned.1.call-done = bf16[128,8,768]{2,1,0:T(8,128)(2,1)} async-done(((bf16[16,8,768]{2,1,0:T(8,128)(2,1)}), bf16[128,8,768]{2,1,0:T(8,128)(2,1)}) %all-gather.2.cloned.1.call-update) | async-done | bytes 1572880 | tf_op jit(solution)/shard_map/all_gather | solution.py:76
  156.1 4.0 %fusion.17 = bf16[512,768]{1,0:T(8,128)(2,1)} fusion(bf16[128,8,768]{2,1,0:T(8,128)(2,1)} %all-gather.2.cloned.1.call-done, f32[512,1024]{1,0:T(8,128)} %get-tuple-element.9, f32[512]{0:T(512)S(1)} %get-tuple-element.5, f32[512]{0:T(512)S(1)} %get-tuple-element.7), kind=kOutput, calls=%fused_computation.32 | convolution fusion | flops 807272448 | bytes 4460544 | tf_op jit(solution)/shard_map/dot_general | solution.py:79
  (17 shorter events, 0.0 us)
Async XLA Ops:
  6.5 1.6 copy-start
  6.5 62.1 %reduce-scatter.5.cloned.1.call-start = ((), (), s32[]{:S(2)}) async-start(), calls=%async_computation.2 | async-start | bytes 1769472 | tf_op jit(solution)/shard_map/reduce_scatter | solution.py:54
  8.2 18.7 %copy-start.1 = (bf16[512,768]{1,0:T(8,128)(2,1)S(1)}, bf16[512,768]{1,0:T(8,128)(2,1)}, u32[]{:S(2)}) copy-start(bf16[512,768]{1,0:T(8,128)(2,1)} %param.4) | copy-start | bytes 2359300
  30.8 98.3 %reduce-scatter.7.cloned.1.call-start = ((), (), s32[]{:S(2)}) async-start(), calls=%async_computation.4 | async-start | bytes 983040
  69.7 12.7 %collective-permute-start = (bf16[16,8,768]{2,1,0:T(8,128)(2,1)S(1)}, bf16[16,8,768]{2,1,0:T(8,128)(2,1)S(1)}, u32[]{:S(2)}, u32[]{:S(2)}) collective-permute-start(bf16[16,8,768]{2,1,0:T(8,128)(2,1)S(1)} %fusion.57), channel_id=1, source_target_pairs={{0,8},{8,16},{16,24},{24,0},{1,9},{9,17},{17,25},{25,1},{2,10},{10... | collective-permute-start | bytes 589832 | tf_op jit(solution)/shard_map/ppermute | solution.py:14
  71.2 19.6 %collective-permute-start.1 = (bf16[16,8,768]{2,1,0:T(8,128)(2,1)S(1)}, bf16[16,8,768]{2,1,0:T(8,128)(2,1)S(1)}, u32[]{:S(2)}, u32[]{:S(2)}) collective-permute-start(bf16[16,8,768]{2,1,0:T(8,128)(2,1)S(1)} %fusion.57), channel_id=1, source_target_pairs={{8,0},{16,8},{24,16},{0,24},{9,1},{17,9},{25,17},{1,25},{10,2},{18... | collective-permute-start | bytes 589832 | tf_op jit(solution)/shard_map/ppermute | solution.py:15
  73.7 17.1 %slice-start = ((s8[18874368]{0:T(1024)(128)(4,1)}), s8[4194304]{0:T(1024)(128)(4,1)S(1)}, s32[]{:S(2)}) async-start(s8[18874368]{0:T(1024)(128)(4,1)} %bitcast.29), calls=%async_computation.5 | async-start | bytes 8388608
  73.7 17.1 %slice-start.1 = ((s8[18874368]{0:T(1024)(128)(4,1)}), s8[4194304]{0:T(1024)(128)(4,1)S(1)}, s32[]{:S(2)}) async-start(s8[18874368]{0:T(1024)(128)(4,1)} %bitcast.29), calls=%async_computation.6 | async-start | bytes 8388608
  73.7 17.1 %slice-start.2 = ((s8[18874368]{0:T(1024)(128)(4,1)}), s8[4194304]{0:T(1024)(128)(4,1)S(1)}, s32[]{:S(2)}) async-start(s8[18874368]{0:T(1024)(128)(4,1)} %bitcast.29), calls=%async_computation.7 | async-start | bytes 8388608
  82.3 8.5 %slice-start.3 = ((s8[18874368]{0:T(1024)(128)(4,1)}), s8[4194304]{0:T(1024)(128)(4,1)S(1)}, s32[]{:S(2)}) async-start(s8[18874368]{0:T(1024)(128)(4,1)} %bitcast.29), calls=%async_computation.8 | async-start | bytes 8388608
  82.3 8.8 %slice-start.4 = ((s8[18874368]{0:T(1024)(128)(4,1)}), s8[2097152]{0:T(1024)(128)(4,1)S(1)}, s32[]{:S(2)}) async-start(s8[18874368]{0:T(1024)(128)(4,1)} %bitcast.29), calls=%async_computation.9 | async-start | bytes 4194304
  82.3 11.3 %collective-permute-start.2 = (bf16[16,8,768]{2,1,0:T(8,128)(2,1)S(1)}, bf16[16,8,768]{2,1,0:T(8,128)(2,1)S(1)}, u32[]{:S(2)}, u32[]{:S(2)}) collective-permute-start(bf16[16,8,768]{2,1,0:T(8,128)(2,1)S(1)} %collective-permute-done), channel_id=1, source_target_pairs={{0,8},{8,16},{16,24},{24,0},{1,9},{9,17},{17,25},{25,1},{2,10},{10... | collective-permute-start | bytes 589832 | tf_op jit(solution)/shard_map/ppermute | solution.py:30
  106.1 50.0 %all-gather.2.cloned.1.call-start = ((), (), s32[]{:S(2)}) async-start(), calls=%async_computation.3 | async-start | bytes 1769472 | tf_op jit(solution)/shard_map/all_gather | solution.py:76
Sparse Core Ops, SparseCore 0:
  30.9 37.6 reduce-scatter.4
  106.2 22.8 reduce-scatter.6
  131.0 25.0 all-gather.1
